TPU v7x, 512 devices: a whole 4x4x16 slice. The times are simulated.
512 devices in a mesh: shot: 4 (over x_lo, core), slab: 128 (over z, y, x_hi).
Axes of the slice: x: 4 (x_hi: 2, x_lo: 2; x = x_hi * 2 + x_lo), y: 4, z: 16, core: 2. Of those that a mesh axis runs over, the one named last changes fastest.
Arguments:
- lame_lambda: float32 [256, 32, 128], P('slab'), may hold values from 0.5 to 1.5
- lame_mu: float32 [256, 32, 128], P('slab'), may hold values from 0.3 to 0.8
- buoyancy: float32 [256, 32, 128], P('slab'), may hold values from 0.5 to 1
- forward_state: float32 [4, 9, 256, 32, 128], P('shot', None, 'slab'), may hold values from -6 to 6
- adjoint_state: float32 [4, 9, 256, 32, 128], P('shot', None, 'slab'), may hold values from -6 to 6
- source_wavelet: float32 [4, 8], P('shot'), may hold values from -20 to 20
- source_cell: int32 [4], P('shot'), may hold values from 0 to 1048575
- residual_traces: float32 [4, 8, 16384], P('shot', None, 'slab'), may hold values from -12 to 12
- receiver_slab: int32 [16384, 1], P('slab'), may hold values from 0 to 127; in each aligned block of 128 rows (0 to 127, 128 to 255, ...) at most 2 rows name the same one
- receiver_cell: int32 [16384], P('slab'), may hold values from 0 to 8191
Outputs:
- adjoint_start: float32 [4, 9, 256, 32, 128], P('shot', None, 'slab')
- lambda_gradient: float32 [256, 32, 128], P('slab', 'shot')
- mu_gradient: float32 [256, 32, 128], P('slab', 'shot')
Inputs may be any that keep to these rules, and one draw needn't show every extreme that they name: `receiver_slab`: among the 128 receivers held by one index of slab, at most 2 lie in any one slab.
All inputs are finite; a program needn't handle non-finite values.
Results may differ from a plain program's by a relative error of at most 0.000067.
Values sent between devices are 32-bit elements; how exact they have to be, the bound alone decides.
No kernel may reach another device: no remote copies, remote signals or barrier semaphores. Data moves between devices by JAX's collectives and lax.ppermute only.
A program may use at most 64 MiB of HBM per device.

v0:
```python
import jax
import jax.numpy as jnp
from jax import lax
from jax.sharding import PartitionSpec as P

TIME_STEP = 0.3


def from_behind(value, axis, steps):
    count = lax.axis_size(axis)
    initial, last = (max(0, -steps), min(count, count - steps))
    return lax.ppermute(value, axis, [(source, source + steps) for source in range(initial, last)])


def next_cell(values, along):
    extent = values.shape[along]
    remainder = lax.slice_in_dim(values, 1, extent, axis=along)
    border = jnp.zeros_like(lax.slice_in_dim(values, 0, 1, axis=along))
    return jnp.concatenate([remainder, border], axis=along)


def prev_cell(values, along):
    extent = values.shape[along]
    remainder = lax.slice_in_dim(values, 0, extent - 1, axis=along)
    border = jnp.zeros_like(lax.slice_in_dim(values, 0, 1, axis=along))
    return jnp.concatenate([border, remainder], axis=along)


def velocity_update(velocity, stress, buoyancy, normal_after, shear_before):
    sigma_xx = stress[:, 0]
    sigma_yy = stress[:, 1]
    sigma_zz = stress[:, 2]
    sigma_xy = stress[:, 3]
    sigma_xz = stress[:, 4]
    sigma_yz = stress[:, 5]
    accel_x = (
        normal_after
        - sigma_xx
        + (sigma_xy - prev_cell(sigma_xy, 2))
        + (sigma_xz - prev_cell(sigma_xz, 3))
    )
    accel_y = (
        sigma_xy
        - shear_before[:, 0]
        + (next_cell(sigma_yy, 2) - sigma_yy)
        + (sigma_yz - prev_cell(sigma_yz, 3))
    )
    accel_z = (
        sigma_xz
        - shear_before[:, 1]
        + (sigma_yz - prev_cell(sigma_yz, 2))
        + (next_cell(sigma_zz, 3) - sigma_zz)
    )
    factor = TIME_STEP * buoyancy
    return jnp.stack(
        [
            velocity[:, 0] - factor * accel_x,
            velocity[:, 1] - factor * accel_y,
            velocity[:, 2] - factor * accel_z,
        ],
        axis=1,
    )


def stress_update(velocity, stress, lame_lambda, lame_mu, speed_before, speeds_after):
    speed_x = velocity[:, 0]
    speed_y = velocity[:, 1]
    speed_z = velocity[:, 2]
    strain_xx = speed_x - speed_before[:, 0]
    strain_yy = speed_y - prev_cell(speed_y, 2)
    strain_zz = speed_z - prev_cell(speed_z, 3)
    strain_xy = next_cell(speed_x, 2) - speed_x + (speeds_after[:, 0] - speed_y)
    strain_xz = next_cell(speed_x, 3) - speed_x + (speeds_after[:, 1] - speed_z)
    strain_yz = next_cell(speed_y, 3) - speed_y + (next_cell(speed_z, 2) - speed_z)
    dilation = strain_xx + strain_yy + strain_zz
    volume_term = lame_lambda * dilation
    twice_mu = 2.0 * lame_mu
    updated = jnp.stack(
        [
            stress[:, 0] - TIME_STEP * (volume_term + twice_mu * strain_xx),
            stress[:, 1] - TIME_STEP * (volume_term + twice_mu * strain_yy),
            stress[:, 2] - TIME_STEP * (volume_term + twice_mu * strain_zz),
            stress[:, 3] - TIME_STEP * (lame_mu * strain_xy),
            stress[:, 4] - TIME_STEP * (lame_mu * strain_xz),
            stress[:, 5] - TIME_STEP * (lame_mu * strain_yz),
        ],
        axis=1,
    )
    return (updated, (strain_xx, strain_yy, strain_zz, strain_xy, strain_xz, strain_yz))


def imaging(strains):
    strain_xx, strain_yy, strain_zz, strain_xy, strain_xz, strain_yz = strains
    dilation = strain_xx + strain_yy + strain_zz
    lambda_term = TIME_STEP * (dilation[0] * dilation[1])
    shear_term = 2.0 * (
        strain_xx[0] * strain_xx[1] + strain_yy[0] * strain_yy[1] + strain_zz[0] * strain_zz[1]
    )
    shear_term = (
        shear_term
        + strain_xy[0] * strain_xy[1]
        + strain_xz[0] * strain_xz[1]
        + strain_yz[0] * strain_yz[1]
    )
    return (lambda_term, TIME_STEP * shear_term)


def shards(
    lame_lambda,
    lame_mu,
    buoyancy,
    forward_state,
    adjoint_state,
    source_wavelet,
    source_cell,
    residual_traces,
    receiver_slab,
    receiver_cell,
):
    planes, rows_y, depth = lame_lambda.shape
    cell_count = planes * rows_y * depth
    steps_total = source_wavelet.shape[1]
    my_slab = lax.axis_index("slab")
    traces = residual_traces[0]
    target_slab = receiver_slab[:, 0]
    targets = (target_slab * cell_count + receiver_cell).astype(jnp.float32)[None, :]
    arrived, landing = (
        lax.all_gather(traces, "slab", axis=1, tiled=True),
        lax.all_gather(targets, "slab", axis=1, tiled=True),
    )
    local_cell = landing[0].astype(jnp.int32) - my_slab * cell_count
    usable = (local_cell >= 0) & (local_cell < cell_count)
    cell_index = jnp.where(usable, local_cell, 0)
    amounts = jnp.where(usable[None, :], arrived, 0.0)
    receiver_push = jnp.zeros((steps_total, cell_count), jnp.float32).at[:, cell_index].add(amounts)
    receiver_push = receiver_push.reshape(steps_total, planes, rows_y, depth)
    source_local = source_cell[0] - my_slab * cell_count
    source_spot = (
        (jnp.arange(cell_count, dtype=jnp.int32) == source_local)
        .astype(jnp.float32)
        .reshape(planes, rows_y, depth)
    )
    wavefields = jnp.concatenate([forward_state, adjoint_state], axis=0)
    grad_lambda = jnp.zeros((planes, rows_y, depth), jnp.float32)
    grad_shear = jnp.zeros((planes, rows_y, depth), jnp.float32)
    for step_index in range(steps_total):
        stress_now = wavefields[:, 3:9]
        normal_next = from_behind(stress_now[:, 0, 0:1], "slab", -1)
        shear_prev = from_behind(stress_now[:, 3:5, planes - 1 : planes], "slab", 1)
        normal_after = jnp.concatenate([stress_now[:, 0, 1:], normal_next], axis=1)
        shear_before = jnp.concatenate([shear_prev, stress_now[:, 3:5, : planes - 1]], axis=2)
        velocity = velocity_update(
            wavefields[:, 0:3], stress_now, buoyancy, normal_after, shear_before
        )
        speed_prev = from_behind(velocity[:, 0:1, planes - 1 : planes], "slab", 1)
        speed_next = from_behind(velocity[:, 1:3, 0:1], "slab", -1)
        speed_before = jnp.concatenate([speed_prev, velocity[:, 0:1, : planes - 1]], axis=2)
        speeds_after = jnp.concatenate([velocity[:, 1:3, 1:], speed_next], axis=2)
        stress, strains = stress_update(
            velocity, stress_now, lame_lambda, lame_mu, speed_before, speeds_after
        )
        lambda_term, shear_term = imaging(strains)
        grad_lambda = grad_lambda + lambda_term
        grad_shear = grad_shear + shear_term
        pushes = jnp.stack([source_spot * source_wavelet[0, step_index], receiver_push[step_index]])
        stress = stress.at[:, 0:3].add(-TIME_STEP * pushes[:, None])
        wavefields = jnp.concatenate([velocity, stress], axis=1)
    lambda_part, shear_part = (
        lax.psum_scatter(grad_lambda, "shot", scatter_dimension=1, tiled=True),
        lax.psum_scatter(grad_shear, "shot", scatter_dimension=1, tiled=True),
    )
    return (wavefields[1:2], lambda_part, shear_part)


def solution(mesh):
    in_specs = (
        P("slab", None, None),
        P("slab", None, None),
        P("slab", None, None),
        P("shot", None, "slab", None, None),
        P("shot", None, "slab", None, None),
        P("shot", None),
        P("shot"),
        P("shot", None, "slab"),
        P("slab", None),
        P("slab"),
    )
    out_specs = (
        P("shot", None, "slab", None, None),
        P("slab", "shot", None),
        P("slab", "shot", None),
    )
    return jax.shard_map(shards, mesh=mesh, in_specs=in_specs, out_specs=out_specs, check_vma=False)
```

profile of v0, /device:TPU:1, one launch (start us, length us, event | category | flops | bytes accessed | tf_op | source)
XLA Modules:
  0.0 1153.6 jit_solution(3995360313206360715)
XLA Ops:
  7.2 0.8 fusion.81
  8.0 5.5 collective-permute-start.2
  13.5 0.8 fusion.298
  14.3 1.3 collective-permute-start
  15.6 0.9 fusion.83
  16.5 0.8 broadcast_multiply_fusion.2
  17.3 0.8 broadcast_multiply_fusion.1
  18.1 1.6 fusion.335
  21.1 304.9 %all-gather.2 = f32[128,1,128]{2,1,0:T(1,128)S(1)} all-gather(f32[1,1,128]{2,1,0:T(1,128)S(1)} %fusion.300), channel_id=2, replica_groups=mesh['shot'=4,'slab'=128] {'slab'}, dimensions={0}, use_global_device_ids=true | all-gather | bytes 66048 | tf_op jit(solution)/shard_map/all_gather | solution.py:129
  326.0 294.9 %all-gather.1 = f32[1,8,16384]{2,1,0:T(8,128)S(1)} all-gather(f32[1,8,128]{2,1,0:T(8,128)} %param.33), channel_id=3, replica_groups=mesh['shot'=4,'slab'=128] {'slab'}, dimensions={2}, use_global_device_ids=true | all-gather | bytes 528384 | tf_op jit(solution)/shard_map/all_gather | solution.py:128
  620.9 5.3 copy.267
  626.3 115.0 %scatter_custom_fusion = f32[8,8192]{0,1:T(8,128)} fusion(s32[16384]{0:T(1024)S(1)} %bitcast.957, f32[16384,8]{1,0:T(8,128)} %copy.267, f32[]{:T(128)} %constant.207.clone.1), kind=kCustom, calls=%fused_computation.9 | custom fusion | flops 131072 | bytes 262656 | tf_op jit(solution)/shard_map/scatter-add | solution.py:135
  741.3 28.7 %slice_reduce_fusion = (f32[8192]{0:T(1024)}, f32[8192]{0:T(1024)S(1)}, f32[8192]{0:T(1024)S(1)}, f32[8192]{0:T(1024)S(1)}, f32[8192]{0:T(1024)S(1)}, /*index=5*...) fusion(f32[8,8192]{0,1:T(8,128)} %scatter_custom_fusion), kind=kLoop, calls=%fused_computation.1 | loop fusion | bytes 524288 | tf_op jit(solution)/shard_map/slice | solution.py:165
  770.6 1.3 broadcast_select_fusion.6
  771.9 1.3 broadcast_select_fusion.4
  773.2 1.3 broadcast_select_fusion.2
  774.8 5.1 collective-permute-start.1
  780.2 1.3 collective-permute-start.4
  782.2 1.3 collective-permute-start.3
  783.6 3.0 collective-permute-done.4
  786.8 3.1 collective-permute-start.6
  790.1 5.8 collective-permute-start.5
  796.1 1.3 collective-permute-start.8
  797.5 5.2 collective-permute-done.8
  802.9 1.3 collective-permute-start.7
  804.3 5.5 collective-permute-start.10
  810.0 3.7 collective-permute-start.9
  814.0 1.3 collective-permute-start.12
  815.3 5.2 collective-permute-done.12
  820.7 1.3 collective-permute-start.11
  822.1 5.5 collective-permute-start.14
  827.8 5.2 collective-permute-start.13
  833.3 1.3 collective-permute-start.16
  834.7 5.2 collective-permute-done.16
  840.0 1.3 collective-permute-start.15
  841.4 5.5 collective-permute-start.18
  847.1 3.7 collective-permute-start.17
  851.0 1.3 collective-permute-start.20
  853.1 4.3 collective-permute-done.20
  857.5 0.7 multiply_multiply_fusion.1
  858.4 4.3 collective-permute-start.22
  863.5 1.3 collective-permute-start.19
  864.8 4.8 collective-permute-done.19
  869.8 1.3 collective-permute-start.24
  871.1 5.7 collective-permute-start.21
  877.7 0.8 multiply_subtract_fusion.4
  878.6 5.1 collective-permute-start.26
  883.8 1.3 collective-permute-start.23
  885.1 5.6 collective-permute-done.23
  891.0 1.3 collective-permute-start.28
  892.3 6.4 collective-permute-start.25
  899.7 0.8 multiply_subtract_fusion.1
  900.5 1.3 collective-permute-start.27
  901.9 6.4 collective-permute-start.29
  909.8 6.0 collective-permute-start.30
  918.0 1.3 collective-permute-start.31
  921.4 3.8 collective-permute-done.31
  925.2 0.9 bitcast_dynamic-update-slice_fusion.2
  926.1 0.9 bitcast_dynamic-update-slice_fusion.1
  927.0 0.9 bitcast_dynamic-update-slice_fusion
  927.9 2.1 fusion.241
  930.1 0.7 fusion.3
  930.8 187.0 %reduce-scatter.3.cloned.1.call-done = f32[2,8,128]{2,1,0:T(8,128)} async-done(((f32[2,32,128]{2,1,0:T(8,128)}), f32[2,8,128]{2,1,0:T(8,128)}) %reduce-scatter.3.cloned.1.call-update) | async-done | bytes 8208 | tf_op jit(solution)/shard_map/reduce_scatter | solution.py:169
  1117.9 28.9 %reduce-scatter.5.cloned.1.call-done = f32[2,8,128]{2,1,0:T(8,128)} async-done(((f32[2,32,128]{2,1,0:T(8,128)}), f32[2,8,128]{2,1,0:T(8,128)}) %reduce-scatter.5.cloned.1.call-update) | async-done | bytes 8208 | tf_op jit(solution)/shard_map/reduce_scatter | solution.py:170
  (193 shorter events, 15.4 us)
Async XLA Ops:
  7.2 1110.7 %reduce-scatter.3.cloned.1.call-start = ((), (), s32[]{:S(2)}) async-start(), calls=%async_computation.2 | async-start | bytes 40960 | tf_op jit(solution)/shard_map/reduce_scatter | solution.py:169
  8.0 766.5 %collective-permute-start.2 = (f32[2,2,1,32,128]{4,3,0,2,1:T(8,128)S(1)}, f32[2,2,1,32,128]{4,3,0,2,1:T(8,128)S(1)}, u32[]{:S(2)}, u32[]{:S(2)}) collective-permute-start(f32[2,2,1,32,128]{4,3,0,2,1:T(8,128)S(1)} %get-tuple-element.218), channel_id=1, source_target_pairs={{0,1},{1,2},{2,3},{3,4},{4,5},{5,6},{6,7},{7,8},{8,9},{9,10},{10,1... | collective-permute-start | bytes 196616 | tf_op jit(solution)/shard_map/ppermute | solution.py:12
  14.3 760.4 %collective-permute-start = (f32[2,1,32,128]{3,2,0,1:T(8,128)S(1)}, f32[2,1,32,128]{3,2,0,1:T(8,128)S(1)}, u32[]{:S(2)}, u32[]{:S(2)}) collective-permute-start(f32[2,1,32,128]{3,2,0,1:T(8,128)S(1)} %get-tuple-element.213), channel_id=1, source_target_pairs={{1,0},{2,1},{3,2},{4,3},{5,4},{6,5},{7,6},{8,7},{9,8},{10,9},{11,1... | collective-permute-start | bytes 98312 | tf_op jit(solution)/shard_map/ppermute | solution.py:12
  741.3 33.2 %copy-start = (f32[1,9,2,32,128]{4,3,2,1,0:T(8,128)S(1)}, f32[1,9,2,32,128]{4,3,2,1,0:T(8,128)}, u32[]{:S(2)}) copy-start(f32[1,9,2,32,128]{4,3,2,1,0:T(8,128)} %param.29) | copy-start | bytes 884740
  741.3 33.2 %copy-start.1 = (f32[1,9,2,32,128]{4,3,2,1,0:T(8,128)S(1)}, f32[1,9,2,32,128]{4,3,2,1,0:T(8,128)}, u32[]{:S(2)}) copy-start(f32[1,9,2,32,128]{4,3,2,1,0:T(8,128)} %param.30) | copy-start | bytes 884740
  770.0 11.5 copy-start.2
  770.0 16.7 %copy-start.3 = (f32[2,32,128]{2,1,0:T(8,128)S(1)}, f32[2,32,128]{2,1,0:T(8,128)}, u32[]{:S(2)}) copy-start(f32[2,32,128]{2,1,0:T(8,128)} %param.27) | copy-start | bytes 98308
  774.8 6.6 collective-permute-start.1
  780.2 6.5 collective-permute-start.4
  782.2 7.6 collective-permute-start.3
  786.8 9.1 collective-permute-start.6
  790.1 7.4 collective-permute-start.5
  796.1 6.5 collective-permute-start.8
  802.9 6.9 collective-permute-start.7
  804.3 9.4 collective-permute-start.10
  810.0 5.3 collective-permute-start.9
  814.0 6.5 collective-permute-start.12
  820.7 6.9 collective-permute-start.11
  822.1 11.0 collective-permute-start.14
  827.8 6.8 collective-permute-start.13
  833.3 6.5 collective-permute-start.16
  840.0 6.9 collective-permute-start.15
  841.4 9.4 collective-permute-start.18
  847.1 6.1 collective-permute-start.17
  850.8 26.0 %copy-start.7 = (f32[8192]{0:T(1024)S(1)}, f32[8192]{0:T(1024)}, u32[]{:S(2)}) copy-start(f32[8192]{0:T(1024)} %get-tuple-element.108) | copy-start | bytes 98308
  851.0 6.5 collective-permute-start.20
  858.4 6.4 collective-permute-start.22
  863.5 6.2 collective-permute-start.19
  869.8 7.9 collective-permute-start.24
  871.1 6.6 collective-permute-start.21
  878.6 6.5 collective-permute-start.26
  883.8 6.9 collective-permute-start.23
  891.0 8.7 collective-permute-start.28
  892.3 7.4 collective-permute-start.25
  900.5 7.8 collective-permute-start.27
  901.9 14.0 %collective-permute-start.29 = (f32[2,2,1,32,128]{4,3,2,0,1:T(8,128)S(1)}, f32[2,2,1,32,128]{4,3,2,0,1:T(8,128)S(1)}, u32[]{:S(2)}, u32[]{:S(2)}) collective-permute-start(f32[2,2,1,32,128]{4,3,2,0,1:T(8,128)S(1)} %fusion.17), channel_id=1, source_target_pairs={{0,1},{1,2},{2,3},{3,4},{4,5},{5,6},{6,7},{7,8},{8,9},{9,10},{10,1... | collective-permute-start | bytes 196616 | tf_op jit(solution)/shard_map/ppermute | solution.py:12
  909.8 9.5 collective-permute-start.30
  918.0 7.2 collective-permute-start.31
  920.1 226.7 %reduce-scatter.5.cloned.1.call-start = ((), (), s32[]{:S(2)}) async-start(), calls=%async_computation.3 | async-start | bytes 40960 | tf_op jit(solution)/shard_map/reduce_scatter | solution.py:170
  921.4 8.6 copy-start.4
  921.4 8.6 copy-start.5
  921.4 8.6 copy-start.6
Sparse Core Ops, SparseCore 0:
  920.2 197.6 reduce-scatter.2
  1121.4 25.3 reduce-scatter.4
where the time goes:
time: 1160 us; the launch traced here: 1150 us
  blocking collectives  600 us (52%)
  waiting for transfers between devices  253 us (22%)
  other arithmetic  141 us (12%)
  starting transfers between devices  103 us (9%)
  local copies, waits for them, and re-layouts  40.4 us (3%)
  between operations  16 us (1%)
    all_gather x1, blocking collectives, shards(): lax.all_gather(targets, 'slab', axis=1, tiled=True)  305 us
    all_gather x1, blocking collectives, shards(): lax.all_gather(traces, 'slab', axis=1, tiled=True)  295 us
    reduce_scatter x1, waiting for transfers between devices, shards(): lax.psum_scatter(grad_lambda, 'shot', scatter_dimension=1, tiled=True)  187 us
    scatter-add x1, other arithmetic, shards(): jnp.zeros((steps_total, cell_count), jnp.float32).at[:, cell_index]  115 us
    ppermute x32, starting transfers between devices, from_behind(): lax.ppermute(value, axis, [(source, source + steps) for source in range(i...  103 us
    ppermute x32, waiting for transfers between devices, from_behind(): lax.ppermute(value, axis, [(source, source + steps) for source in range(i...  37.4 us
    reduce_scatter x1, waiting for transfers between devices, shards(): lax.psum_scatter(grad_shear, 'shot', scatter_dimension=1, tiled=True)  28.9 us
    slice x1, local copies, waits for them, and re-layouts, shards(): receiver_push[step_index]  28.7 us
  transfers between devices with their start and end apart: 34, of which 11 were waited for; matrix products, arithmetic and copies ran while one was open for 15% of the time, Pallas kernels for 0%

commit v1 on v0

--- a/solution.py
+++ b/solution.py
@@ -126,7 +126,9 @@
     targets = (target_slab * cell_count + receiver_cell).astype(jnp.float32)[None, :]
     arrived, landing = (
         lax.all_gather(traces, "slab", axis=1, tiled=True),
-        lax.all_gather(targets, "slab", axis=1, tiled=True),
+        jnp.concatenate(
+            lax.all_to_all(jnp.stack([targets] * lax.axis_size("slab")), "slab", 0, 0), axis=1
+        ),
     )
     local_cell = landing[0].astype(jnp.int32) - my_slab * cell_count
     usable = (local_cell >= 0) & (local_cell < cell_count)

time: 1160 us -> 837 us (0.72)
  blocking collectives: 600 us -> 302 us
  waiting for transfers between devices: 253 us -> 207 us
  starting transfers between devices: 103 us -> 125 us
    all_gather x1 -> x0, blocking collectives: 305 us -> none  [shards(): lax.all_gather(targets, 'slab', axis=1, tiled=True)]
    reduce_scatter x1, waiting for transfers between devices: 187 us -> 136 us  [shards(): lax.psum_scatter(grad_lambda, 'shot', scatter_dimension=1, tiled=True)]
    all_to_all x0 -> x1, starting transfers between devices: none -> 23 us  [shards(): lax.all_to_all(jnp.stack([targets] * lax.axis_size('slab')), 'slab', 0, 0)]
  transfers between devices with their start and end apart: 34 -> 35, of which waited for: 11 -> 14; matrix products, arithmetic and copies ran while one was open for 15% -> 4% of each run, Pallas kernels for 0% -> 0%
where the time goes in v1:
time: 837 us; the launch traced here: 835 us
  blocking collectives  302 us (36%)
  waiting for transfers between devices  207 us (25%)
  other arithmetic  144 us (17%)
  starting transfers between devices  125 us (15%)
  local copies, waits for them, and re-layouts  41.2 us (5%)
  between operations  16 us (2%)
    all_gather x1, blocking collectives, shards(): lax.all_gather(traces, 'slab', axis=1, tiled=True)  302 us
    reduce_scatter x1, waiting for transfers between devices, shards(): lax.psum_scatter(grad_lambda, 'shot', scatter_dimension=1, tiled=True)  136 us
    scatter-add x1, other arithmetic, shards(): jnp.zeros((steps_total, cell_count), jnp.float32).at[:, cell_index]  115 us
    ppermute x32, starting transfers between devices, from_behind(): lax.ppermute(value, axis, [(source, source + steps) for source in range(i...  102 us
    ppermute x32, waiting for transfers between devices, from_behind(): lax.ppermute(value, axis, [(source, source + steps) for source in range(i...  41.5 us
    reduce_scatter x1, waiting for transfers between devices, shards(): lax.psum_scatter(grad_shear, 'shot', scatter_dimension=1, tiled=True)  28.9 us
    slice x1, local copies, waits for them, and re-layouts, shards(): receiver_push[step_index]  28.8 us
    all_to_all x1, starting transfers between devices, shards(): lax.all_to_all(jnp.stack([targets] * lax.axis_size('slab')), 'slab', 0, 0)  23 us
  transfers between devices with their start and end apart: 35, of which 14 were waited for; matrix products, arithmetic and copies ran while one was open for 4% of the time, Pallas kernels for 0%

profile of v1, /device:TPU:1, one launch (start us, length us, event | category | flops | bytes accessed | tf_op | source)
XLA Modules:
  0.0 835.4 jit_solution(13918147381872450882)
XLA Ops:
  7.2 0.9 fusion.81
  8.1 5.5 collective-permute-start.2
  14.4 1.3 collective-permute-start
  17.0 23.0 %all-to-all-start = ((f32[128,1,128]{2,1,0:T(1,128)}), f32[128,1,128]{2,1,0:T(1,128)S(1)}, u32[]{:S(2)}, u32[]{:S(2)}) async-start(f32[128,1,128]{2,1,0:T(1,128)} %stack.322), calls=%async_computation | async-start | bytes 131072 | tf_op jit(solution)/shard_map/all_to_all | solution.py:130
  40.0 0.9 fusion.83
  42.5 1.6 fusion.334
  44.8 302.1 %all-gather = f32[1,8,16384]{2,1,0:T(8,128)S(1)} all-gather(f32[1,8,128]{2,1,0:T(8,128)} %param.33), channel_id=2, replica_groups=mesh['shot'=4,'slab'=128] {'slab'}, dimensions={2}, use_global_device_ids=true | all-gather | bytes 528384 | tf_op jit(solution)/shard_map/all_gather | solution.py:128
  346.9 1.3 broadcast_select_fusion.1
  348.2 1.3 broadcast_select_fusion.6
  349.5 1.8 broadcast_select_fusion.4
  351.3 1.9 broadcast_select_fusion.2
  353.2 1.3 broadcast_select_fusion
  354.4 0.9 fusion.65
  355.5 1.3 collective-permute-start.1
  357.0 1.3 collective-permute-start.4
  359.0 4.5 collective-permute-done.4
  363.6 3.3 collective-permute-start.6
  367.0 1.3 collective-permute-done.6
  368.4 5.3 copy.267
  373.8 115.0 %scatter_custom_fusion = f32[8,8192]{0,1:T(8,128)} fusion(s32[16384]{0:T(1024)S(1)} %bitcast.953, f32[16384,8]{1,0:T(8,128)} %copy.267, f32[]{:T(128)} %constant.207.clone.1), kind=kCustom, calls=%fused_computation.9 | custom fusion | flops 131072 | bytes 262656 | tf_op jit(solution)/shard_map/scatter-add | solution.py:137
  488.8 28.8 %slice_reduce_fusion = (f32[8192]{0:T(1024)}, f32[8192]{0:T(1024)S(1)}, f32[8192]{0:T(1024)S(1)}, f32[8192]{0:T(1024)S(1)}, f32[8192]{0:T(1024)S(1)}, /*index=5*...) fusion(f32[8,8192]{0,1:T(8,128)} %scatter_custom_fusion), kind=kLoop, calls=%fused_computation.1 | loop fusion | bytes 524288 | tf_op jit(solution)/shard_map/slice | solution.py:167
  517.6 1.3 collective-permute-start.3
  519.2 1.3 collective-permute-start.8
  520.6 3.7 collective-permute-done.3
  524.3 5.8 collective-permute-start.5
  530.2 0.9 collective-permute-done.5
  531.3 1.3 collective-permute-start.7
  532.7 5.8 collective-permute-start.10
  538.7 5.8 collective-permute-start.9
  544.8 1.3 collective-permute-start.12
  546.1 5.2 collective-permute-done.12
  551.5 1.3 collective-permute-start.11
  552.9 5.5 collective-permute-start.14
  558.6 4.7 collective-permute-start.13
  563.6 1.3 collective-permute-start.16
  565.0 5.2 collective-permute-done.16
  570.3 1.3 collective-permute-start.15
  571.8 5.5 collective-permute-start.18
  577.4 4.9 collective-permute-start.17
  582.4 1.3 collective-permute-start.20
  584.0 5.0 collective-permute-done.20
  589.9 4.3 collective-permute-start.22
  594.9 1.3 collective-permute-start.19
  596.3 4.8 collective-permute-done.19
  601.3 1.3 collective-permute-start.24
  602.6 5.5 collective-permute-start.21
  609.1 0.8 multiply_subtract_fusion.4
  610.0 5.3 collective-permute-start.26
  615.5 1.3 collective-permute-start.23
  616.8 5.9 collective-permute-done.23
  622.9 1.3 collective-permute-start.28
  624.2 5.9 collective-permute-start.25
  632.1 1.3 collective-permute-start.27
  633.4 6.4 collective-permute-start.29
  641.3 6.0 collective-permute-start.30
  649.5 1.3 collective-permute-start.31
  652.3 4.6 collective-permute-done.31
  656.9 0.9 bitcast_dynamic-update-slice_fusion.2
  657.8 0.9 bitcast_dynamic-update-slice_fusion.1
  658.7 0.9 bitcast_dynamic-update-slice_fusion
  659.6 2.1 fusion.241
  661.8 0.9 fusion.4
  663.4 136.2 %reduce-scatter.3.cloned.1.call-done = f32[2,8,128]{2,1,0:T(8,128)} async-done(((f32[2,32,128]{2,1,0:T(8,128)}), f32[2,8,128]{2,1,0:T(8,128)}) %reduce-scatter.3.cloned.1.call-update) | async-done | bytes 8208 | tf_op jit(solution)/shard_map/reduce_scatter | solution.py:171
  799.6 28.9 %reduce-scatter.5.cloned.1.call-done = f32[2,8,128]{2,1,0:T(8,128)} async-done(((f32[2,32,128]{2,1,0:T(8,128)}), f32[2,8,128]{2,1,0:T(8,128)}) %reduce-scatter.5.cloned.1.call-update) | async-done | bytes 8208 | tf_op jit(solution)/shard_map/reduce_scatter | solution.py:172
  (199 shorter events, 18.8 us)
Async XLA Ops:
  7.2 348.2 %copy-start = (f32[1,9,2,32,128]{4,3,2,1,0:T(8,128)S(1)}, f32[1,9,2,32,128]{4,3,2,1,0:T(8,128)}, u32[]{:S(2)}) copy-start(f32[1,9,2,32,128]{4,3,2,1,0:T(8,128)} %param.29) | copy-start | bytes 884740
  7.2 348.2 %copy-start.1 = (f32[1,9,2,32,128]{4,3,2,1,0:T(8,128)S(1)}, f32[1,9,2,32,128]{4,3,2,1,0:T(8,128)}, u32[]{:S(2)}) copy-start(f32[1,9,2,32,128]{4,3,2,1,0:T(8,128)} %param.30) | copy-start | bytes 884740
  7.2 351.2 %copy-start.2 = (f32[2,32,128]{2,1,0:T(8,128)S(1)}, f32[2,32,128]{2,1,0:T(8,128)}, u32[]{:S(2)}) copy-start(f32[2,32,128]{2,1,0:T(8,128)} %param.26) | copy-start | bytes 98308
  8.1 355.5 %copy-start.3 = (f32[2,32,128]{2,1,0:T(8,128)S(1)}, f32[2,32,128]{2,1,0:T(8,128)}, u32[]{:S(2)}) copy-start(f32[2,32,128]{2,1,0:T(8,128)} %param.27) | copy-start | bytes 98308
  8.1 346.3 %collective-permute-start.2 = (f32[2,2,1,32,128]{4,3,0,2,1:T(8,128)S(1)}, f32[2,2,1,32,128]{4,3,0,2,1:T(8,128)S(1)}, u32[]{:S(2)}, u32[]{:S(2)}) collective-permute-start(f32[2,2,1,32,128]{4,3,0,2,1:T(8,128)S(1)} %get-tuple-element.218), channel_id=1, source_target_pairs={{0,1},{1,2},{2,3},{3,4},{4,5},{5,6},{6,7},{7,8},{8,9},{9,10},{10,1... | collective-permute-start | bytes 196616 | tf_op jit(solution)/shard_map/ppermute | solution.py:12
  14.4 341.0 %collective-permute-start = (f32[2,1,32,128]{3,2,0,1:T(8,128)S(1)}, f32[2,1,32,128]{3,2,0,1:T(8,128)S(1)}, u32[]{:S(2)}, u32[]{:S(2)}) collective-permute-start(f32[2,1,32,128]{3,2,0,1:T(8,128)S(1)} %get-tuple-element.213), channel_id=1, source_target_pairs={{1,0},{2,1},{3,2},{4,3},{5,4},{6,5},{7,6},{8,7},{9,8},{10,9},{11,1... | collective-permute-start | bytes 98312 | tf_op jit(solution)/shard_map/ppermute | solution.py:12
  17.0 351.3 %all-to-all-start = ((f32[128,1,128]{2,1,0:T(1,128)}), f32[128,1,128]{2,1,0:T(1,128)S(1)}, u32[]{:S(2)}, u32[]{:S(2)}) async-start(f32[128,1,128]{2,1,0:T(1,128)} %stack.322), calls=%async_computation | async-start | bytes 131072 | tf_op jit(solution)/shard_map/all_to_all | solution.py:130
  40.0 759.7 %reduce-scatter.3.cloned.1.call-start = ((), (), s32[]{:S(2)}) async-start(), calls=%async_computation.3 | async-start | bytes 40960 | tf_op jit(solution)/shard_map/reduce_scatter | solution.py:171
  355.5 2.8 collective-permute-start.1
  357.0 6.5 collective-permute-start.4
  363.6 4.6 collective-permute-start.6
  517.6 6.6 collective-permute-start.3
  519.2 11.9 %collective-permute-start.8 = (f32[2,2,1,32,128]{4,3,0,2,1:T(8,128)S(1)}, f32[2,2,1,32,128]{4,3,0,2,1:T(8,128)S(1)}, u32[]{:S(2)}, u32[]{:S(2)}) collective-permute-start(f32[2,2,1,32,128]{4,3,0,2,1:T(8,128)S(1)} %get-tuple-element.330), channel_id=1, source_target_pairs={{1,0},{2,1},{3,2},{4,3},{5,4},{6,5},{7,6},{8,7},{9,8},{10,9},{11,1... | collective-permute-start | bytes 196616 | tf_op jit(solution)/shard_map/ppermute | solution.py:12
  524.3 6.8 collective-permute-start.5
  531.3 7.2 collective-permute-start.7
  532.7 11.8 %collective-permute-start.10 = (f32[2,2,1,32,128]{4,3,0,2,1:T(8,128)S(1)}, f32[2,2,1,32,128]{4,3,0,2,1:T(8,128)S(1)}, u32[]{:S(2)}, u32[]{:S(2)}) collective-permute-start(f32[2,2,1,32,128]{4,3,0,2,1:T(8,128)S(1)} %fusion.47), channel_id=1, source_target_pairs={{0,1},{1,2},{2,3},{3,4},{4,5},{5,6},{6,7},{7,8},{8,9},{9,10},{10,1... | collective-permute-start | bytes 196616 | tf_op jit(solution)/shard_map/ppermute | solution.py:12
  538.7 7.4 collective-permute-start.9
  544.8 6.5 collective-permute-start.12
  551.3 19.0 %copy-start.6 = (f32[1,2,32,128]{3,2,1,0:T(8,128)S(1)}, f32[1,2,32,128]{3,2,1,0:T(8,128)}, u32[]{:S(2)}) copy-start(f32[1,2,32,128]{3,2,1,0:T(8,128)} %get-tuple-element.369) | copy-start | bytes 98308
  551.5 6.9 collective-permute-start.11
  552.9 10.5 %collective-permute-start.14 = (f32[2,2,1,32,128]{4,3,0,2,1:T(8,128)S(1)}, f32[2,2,1,32,128]{4,3,0,2,1:T(8,128)S(1)}, u32[]{:S(2)}, u32[]{:S(2)}) collective-permute-start(f32[2,2,1,32,128]{4,3,0,2,1:T(8,128)S(1)} %fusion.41), channel_id=1, source_target_pairs={{0,1},{1,2},{2,3},{3,4},{4,5},{5,6},{6,7},{7,8},{8,9},{9,10},{10,1... | collective-permute-start | bytes 196616 | tf_op jit(solution)/shard_map/ppermute | solution.py:12
  558.5 25.2 %copy-start.8 = (f32[1,2,32,128]{3,2,1,0:T(8,128)S(1)}, f32[1,2,32,128]{3,2,1,0:T(8,128)}, u32[]{:S(2)}) copy-start(f32[1,2,32,128]{3,2,1,0:T(8,128)} %broadcast_select_fusion.1) | copy-start | bytes 98308
  558.6 6.3 collective-permute-start.13
  563.6 6.5 collective-permute-start.16
  570.1 19.6 %copy-start.5 = (f32[1,2,32,128]{3,2,1,0:T(8,128)S(1)}, f32[1,2,32,128]{3,2,1,0:T(8,128)}, u32[]{:S(2)}) copy-start(f32[1,2,32,128]{3,2,1,0:T(8,128)} %get-tuple-element.368) | copy-start | bytes 98308
  570.3 6.9 collective-permute-start.15
  571.8 10.5 %collective-permute-start.18 = (f32[2,2,1,32,128]{4,3,0,2,1:T(8,128)S(1)}, f32[2,2,1,32,128]{4,3,0,2,1:T(8,128)S(1)}, u32[]{:S(2)}, u32[]{:S(2)}) collective-permute-start(f32[2,2,1,32,128]{4,3,0,2,1:T(8,128)S(1)} %fusion.35), channel_id=1, source_target_pairs={{0,1},{1,2},{2,3},{3,4},{4,5},{5,6},{6,7},{7,8},{8,9},{9,10},{10,1... | collective-permute-start | bytes 196616 | tf_op jit(solution)/shard_map/ppermute | solution.py:12
  577.4 6.6 collective-permute-start.17
  582.3 25.8 %copy-start.7 = (f32[1,2,32,128]{3,2,1,0:T(8,128)S(1)}, f32[1,2,32,128]{3,2,1,0:T(8,128)}, u32[]{:S(2)}) copy-start(f32[1,2,32,128]{3,2,1,0:T(8,128)} %broadcast_select_fusion) | copy-start | bytes 98308
  582.3 25.8 %copy-start.9 = (f32[8192]{0:T(1024)S(1)}, f32[8192]{0:T(1024)}, u32[]{:S(2)}) copy-start(f32[8192]{0:T(1024)} %get-tuple-element.108) | copy-start | bytes 98308
  582.4 6.5 collective-permute-start.20
  589.9 6.4 collective-permute-start.22
  594.9 6.2 collective-permute-start.19
  601.3 7.8 collective-permute-start.24
  602.6 6.5 collective-permute-start.21
  610.0 6.7 collective-permute-start.26
  615.5 7.2 collective-permute-start.23
  622.9 8.3 collective-permute-start.28
  624.2 7.0 collective-permute-start.25
  632.1 7.8 collective-permute-start.27
  633.4 14.0 %collective-permute-start.29 = (f32[2,2,1,32,128]{4,3,2,0,1:T(8,128)S(1)}, f32[2,2,1,32,128]{4,3,2,0,1:T(8,128)S(1)}, u32[]{:S(2)}, u32[]{:S(2)}) collective-permute-start(f32[2,2,1,32,128]{4,3,2,0,1:T(8,128)S(1)} %fusion.17), channel_id=1, source_target_pairs={{0,1},{1,2},{2,3},{3,4},{4,5},{5,6},{6,7},{7,8},{8,9},{9,10},{10,1... | collective-permute-start | bytes 196616 | tf_op jit(solution)/shard_map/ppermute | solution.py:12
  641.3 9.5 %collective-permute-start.30 = (f32[2,1,1,32,128]{4,3,2,0,1:T(8,128)S(1)}, f32[2,1,1,32,128]{4,3,2,0,1:T(8,128)S(1)}, u32[]{:S(2)}, u32[]{:S(2)}) collective-permute-start(f32[2,1,1,32,128]{4,3,2,0,1:T(8,128)S(1)} %get-tuple-element.340), channel_id=1, source_target_pairs={{0,1},{1,2},{2,3},{3,4},{4,5},{5,6},{6,7},{7,8},{8,9},{9,10},{10,1... | collective-permute-start | bytes 98312 | tf_op jit(solution)/shard_map/ppermute | solution.py:12
  649.5 7.4 collective-permute-start.31
  651.6 177.0 %reduce-scatter.5.cloned.1.call-start = ((), (), s32[]{:S(2)}) async-start(), calls=%async_computation.4 | async-start | bytes 40960 | tf_op jit(solution)/shard_map/reduce_scatter | solution.py:172
  652.3 9.5 %copy-start.4 = (f32[2,1,2,32,128]{4,3,2,0,1:T(8,128)S(1)}, f32[2,1,2,32,128]{4,3,2,0,1:T(8,128)}, u32[]{:S(2)}) copy-start(f32[2,1,2,32,128]{4,3,2,0,1:T(8,128)} %get-tuple-element.123) | copy-start | bytes 196612
Sparse Core Ops, SparseCore 0:
  651.7 147.8 reduce-scatter.2
  803.2 25.3 reduce-scatter.4
